TPU v7x, 256 devices: a whole 4x4x8 slice. The times are simulated.
256 devices in a mesh: tm: 32 (over y, z), space: 8 (over x, core).
Axes of the slice: x: 4, y: 4, z: 8, core: 2. Of those that a mesh axis runs over, the one named last changes fastest.
Arguments:
- inverse_factor: bfloat16 [2, 32, 4096, 4096], P(None, 'tm', 'space'), may hold values from -1.5 to 1.5, as said below
- tile_mask: int32 [32, 32], replicated, may hold values 0 or 1
- carry_rate: float32 [32, 4096, 2], P('tm', 'space'), may hold values from 0 to 1
- right_side: float32 [32, 4096, 2, 128], P('tm', 'space'), may hold values from -1.5 to 1.5
- arrow_rows: bfloat16 [32, 4096, 2, 512], P('tm', 'space'), may hold values from -0.0625 to 0.0625
- fixed_rhs: float32 [2, 512, 128], P(None, ('tm', 'space')), may hold values from -6 to 6
- tip_factor: bfloat16 [2, 512, 512], replicated, may hold values from -1 to 1, as said below
Outputs:
- solution: float32 [32, 4096, 2, 128], P('tm', 'space')
- fixed_solution: float32 [2, 512, 128], P(None, ('tm', 'space'))
Inputs may be any that keep to these rules, and one draw needn't show every extreme that they name: `tile_mask`: 1 marks a tile that may be nonzero. `inverse_factor`: only entries on or below the diagonal are read. `tip_factor`: only entries on or below the diagonal are read.
All inputs are finite; a program needn't handle non-finite values.
Results may differ from a plain program's by a relative error of at most 0.022.
Values may be sent and summed in bfloat16 or wider, within the bound.
No kernel may reach another device: no remote copies, remote signals or barrier semaphores. Data moves between devices by JAX's collectives and lax.ppermute only.
A program may use at most 320 MiB of HBM per device.

v0:
```python
import jax
import jax.numpy as jnp
from jax import lax
from jax.sharding import PartitionSpec as P

TILE = 128


def carried_in(shard, axis, join, neutral, backward):
    count = lax.axis_size(axis)
    place = lax.axis_index(axis)
    ahead = count - 1 - place if backward else place
    gathered = jax.tree.map(
        lambda a, kind: lax.all_gather(a.astype(kind), axis), shard, (jnp.bfloat16, jnp.bfloat16)
    )
    state = jax.tree.map(lambda a, e: jnp.zeros_like(a) + jnp.asarray(e, a.dtype), shard, neutral)

    def one(turn, state):
        source = count - 1 - turn if backward else turn
        return join(
            state,
            jax.tree.map(
                lambda a, own: lax.dynamic_index_in_dim(a, source, 0, False).astype(own.dtype),
                gathered,
                shard,
            ),
        )

    return lax.fori_loop(0, ahead, one, state)


def combine(earlier, latter):
    rate_new = latter[0] * earlier[0]
    rest = tuple(
        (value_l + latter[0] * value_e for value_l, value_e in zip(latter[1:], earlier[1:]))
    )
    return (rate_new,) + rest


def tile_keep(tile_table, row_start, row_total, col_total):
    tile_count = tile_table.shape[0]
    tile_ids = jnp.arange(tile_count, dtype=jnp.int32)
    row_index = row_start + jnp.arange(row_total, dtype=jnp.int32)
    col_index = jnp.arange(col_total, dtype=jnp.int32)
    row_onehot = (row_index[:, None] // TILE == tile_ids[None, :]).astype(jnp.float32)
    col_onehot = (col_index[:, None] // TILE == tile_ids[None, :]).astype(jnp.float32)
    marked = jnp.dot(jnp.dot(row_onehot, tile_table.astype(jnp.float32)), col_onehot.T)
    return (marked > 0.5) & (row_index[:, None] >= col_index[None, :])


def on_device(inverse_factor, tile_mask, carry_rate, right_side, arrow_rows, fixed_rhs, tip_factor):
    row_count = right_side.shape[1]
    node_total = inverse_factor.shape[3]
    row_start = lax.axis_index("space") * row_count
    tile_table = jnp.maximum(tile_mask, jnp.eye(tile_mask.shape[0], dtype=jnp.int32))
    weights = inverse_factor[:, 0]
    bf_zero = jnp.zeros((), jnp.bfloat16)
    rate_col = carry_rate[0][:, :, None]
    source = right_side[0]
    unit_rate = jnp.ones_like(rate_col)
    earlier_sum = carried_in(
        (rate_col, source), "tm", combine, (unit_rate, jnp.zeros_like(source)), False
    )
    forward = source + rate_col * earlier_sum[1]
    forward_b = forward.astype(jnp.bfloat16)
    row_keep = tile_keep(tile_table, row_start, row_count, node_total)
    masked_rows = jnp.where(row_keep[None], weights, bf_zero)
    block = masked_rows
    inner_rows = jnp.einsum(
        "hrn,nhk->rhk",
        block,
        lax.all_gather(forward_b, "space", axis=0, tiled=True),
        preferred_element_type=jnp.float32,
    ).astype(jnp.bfloat16)
    block = masked_rows
    scaled = lax.psum_scatter(
        jnp.einsum("hrn,rhk->nhk", block, inner_rows, preferred_element_type=jnp.float32).astype(
            jnp.bfloat16
        ),
        "space",
        scatter_dimension=0,
        tiled=True,
    ).astype(jnp.float32)
    arrow_part = arrow_rows[0]
    coupling = jnp.einsum("rhf,rhk->hfk", arrow_part, forward_b, preferred_element_type=jnp.float32)
    share_rows = fixed_rhs.shape[1]
    share_start = lax.axis_index(("tm", "space")) * share_rows
    contrib = -coupling
    own_part = lax.dynamic_slice_in_dim(contrib, share_start, share_rows, 1) + fixed_rhs
    contrib = lax.dynamic_update_slice_in_dim(contrib, own_part, share_start, 1)
    fixed_forward = lax.psum(contrib, ("tm", "space")).astype(jnp.bfloat16)
    fixed_total = tip_factor.shape[1]
    fixed_index = jnp.arange(fixed_total, dtype=jnp.int32)
    lower_tri = fixed_index[:, None] >= fixed_index[None, :]
    tip_lower = jnp.where(lower_tri[None], tip_factor, bf_zero)
    tip_inner = jnp.einsum(
        "hij,hjk->hik", tip_lower, fixed_forward, preferred_element_type=jnp.float32
    ).astype(jnp.bfloat16)
    fixed_solution = jnp.einsum(
        "hij,hik->hjk", tip_lower, tip_inner, preferred_element_type=jnp.float32
    )
    fixed_own = lax.dynamic_slice_in_dim(fixed_solution, share_start, share_rows, 1)
    fixed_b = fixed_solution.astype(jnp.bfloat16)
    carried = scaled - jnp.einsum(
        "rhf,hfk->rhk", arrow_part, fixed_b, preferred_element_type=jnp.float32
    )
    following = carried_in(
        (rate_col, rate_col * carried), "tm", combine, (unit_rate, jnp.zeros_like(carried)), True
    )
    solution = carried + following[1]
    return (solution[None], fixed_own)


def solution(mesh):
    placed = (
        P(None, "tm", "space", None),
        P(),
        P("tm", "space", None),
        P("tm", "space", None, None),
        P("tm", "space", None, None),
        P(None, ("tm", "space"), None),
        P(),
    )
    return jax.shard_map(
        on_device,
        mesh=mesh,
        in_specs=placed,
        out_specs=(P("tm", "space", None, None), P(None, ("tm", "space"), None)),
        check_vma=False,
    )
```

profile of v0, /device:TPU:2, one launch (start us, length us, event | category | flops | bytes accessed | tf_op | source)
XLA Modules:
  0.0 596.0 jit_solution(12626880782622736189)
XLA Ops:
  11.1 52.1 %all-gather = bf16[32,512,2]{1,2,0:T(2,128)(2,1)S(1)} all-gather(bf16[1,512,2]{1,2,0:T(2,128)(2,1)S(1)} %convert_element_type.103), channel_id=2, replica_groups=mesh['tm'=32,'space'=8] {'tm'}, dimensions={0}, use_global_device_ids=true | all-gather | bytes 67584 | tf_op jit(solution)/shard_map/all_gather | solution.py:14
  63.2 3.3 copy.37
  66.6 46.1 %all-gather.6.cloned.1.call-done = bf16[32,512,2,128]{3,1,2,0:T(8,128)(2,1)} async-done(((bf16[1,512,2,128]{3,1,2,0:T(8,128)(2,1)}), bf16[32,512,2,128]{3,1,2,0:T(8,128)(2,1)}) %all-gather.6.cloned.1.call-update) | async-done | bytes 8388624 | tf_op jit(solution)/shard_map/all_gather | solution.py:14
  114.4 4.2 fusion
  118.6 154.2 %all-gather.8.cloned.1.call-done = bf16[4096,2,128]{0,2,1:T(8,128)(2,1)} async-done(((bf16[512,2,128]{0,2,1:T(8,128)(2,1)}), bf16[4096,2,128]{0,2,1:T(8,128)(2,1)}) %all-gather.8.cloned.1.call-update) | async-done | bytes 2097168 | tf_op jit(solution)/shard_map/all_gather | solution.py:72
  272.7 13.2 %fusion.4 = bf16[4096,2,128]{0,2,1:T(8,128)(2,1)} fusion(bf16[2,1,512,4096]{3,2,1,0:T(8,128)(2,1)} %param.11, pred[512,4096]{1,0:T(8,128)(4,1)} %fusion, bf16[4096,2,128]{0,2,1:T(8,128)(2,1)} %all-gather.8.cloned.1.call-done), kind=kOutput, calls=%fused_computation.12 | convolution fusion | flops 2157051904 | bytes 14680064 | tf_op jit(solution)/shard_map/hrn,rhk->nhk/dot_general | solution.py:77
  287.8 78.9 %all-reduce.1 = bf16[2,512,128]{1,2,0:T(8,128)(2,1)S(1)} all-reduce(f32[2,512,128]{1,2,0:T(8,128)S(1)} %dynamic_update_slice.3), channel_id=1, replica_groups=mesh['tm'=32,'space'=8] {'tm','space'}, use_global_device_ids=true, to_apply=%region_3.4 | all-reduce | flops 131072 | bytes 786432 | tf_op jit(solution)/shard_map/psum | solution.py:91
  366.7 2.3 fusion.9
  369.0 2.1 multiply_convert_fusion
  371.8 102.9 %all-gather.10.cloned.1.call-done = bf16[16384,2,128]{0,2,1:T(8,128)(2,1)} async-done(((bf16[512,2,128]{0,2,1:T(8,128)(2,1)}), bf16[16384,2,128]{0,2,1:T(8,128)(2,1)}) %all-gather.10.cloned.1.call-update) | async-done | bytes 8388624 | tf_op jit(solution)/shard_map/all_gather | solution.py:14
  474.7 21.1 %copy.52 = bf16[16384,2,128]{2,1,0:T(2,128)(2,1)} copy(bf16[16384,2,128]{0,2,1:T(8,128)(2,1)} %all-gather.10.cloned.1.call-done) | data formatting | bytes 16777216 | tf_op jit(solution)/shard_map/while | solution.py:29
  495.9 92.2 %while.27 = (s32[]{:T(128)}, f32[512,2,128]{2,1,0:T(2,128)S(1)}, s32[]{:T(128)}, bf16[32,512,2,128]{3,2,1,0:T(2,128)(2,1)}, bf16[32,512,2,1]{2,1,3,0:T(8,128)(2,...) while((s32[]{:T(128)}, f32[512,2,128]{2,1,0:T(2,128)S(1)}, s32[]{:T(128)}, ...), condition=%wide.region_5.6_spmd, body=%wide.region_4.5_spmd.sunk | while | flops 394246 | bytes 1321107 | solution.py:29
  499.8 2.0 convert_add_fusion.5
  502.8 2.0 convert_add_fusion.5
  505.8 2.0 convert_add_fusion.5
  508.8 2.0 convert_add_fusion.5
  511.7 2.0 convert_add_fusion.5
  520.7 2.0 convert_add_fusion.5
  523.6 2.0 convert_add_fusion.5
  526.6 2.0 convert_add_fusion.5
  529.6 2.0 convert_add_fusion.5
  538.5 2.0 convert_add_fusion.5
  541.5 2.0 convert_add_fusion.5
  544.5 2.0 convert_add_fusion.5
  (88 shorter events, 76.4 us)
Async XLA Ops:
  7.2 279.1 %copy-start = (bf16[1,512,2,512]{3,2,1,0:T(2,128)(2,1)S(1)}, bf16[1,512,2,512]{3,2,1,0:T(2,128)(2,1)}, u32[]{:S(2)}) copy-start(bf16[1,512,2,512]{3,2,1,0:T(2,128)(2,1)} %param.15) | copy-start | bytes 3145732
  7.2 105.5 %all-gather.6.cloned.1.call-start = ((), (), s32[]{:S(2)}) async-start(), calls=%async_computation.1 | async-start | bytes 8650752 | tf_op jit(solution)/shard_map/all_gather | solution.py:14
  9.1 263.6 %all-gather.8.cloned.1.call-start = ((), (), s32[]{:S(2)}) async-start(), calls=%async_computation.2 | async-start | bytes 2359296 | tf_op jit(solution)/shard_map/all_gather | solution.py:72
  112.8 0.7 copy-start.2
  112.8 1.6 copy-start.4
  114.3 254.7 %reduce-scatter.2.cloned.1.call-start = ((), (), s32[]{:S(2)}) async-start(), calls=%async_computation.3 | async-start | bytes 2359296 | tf_op jit(solution)/shard_map/reduce_scatter | solution.py:76
  118.6 167.5 %copy-start.3 = (f32[2,2,128]{2,1,0:T(2,128)S(1)}, f32[2,2,128]{2,1,0:T(2,128)}, u32[]{:S(2)}) copy-start(f32[2,2,128]{2,1,0:T(2,128)} %param.16) | copy-start | bytes 6148
  118.6 167.7 %copy-start.1 = (bf16[512,2,128]{0,2,1:T(8,128)(2,1)S(1)}, bf16[512,2,128]{0,2,1:T(8,128)(2,1)}, u32[]{:S(2)}) copy-start(bf16[512,2,128]{0,2,1:T(8,128)(2,1)} %fusion.19) | copy-start | bytes 786436
  286.0 188.7 %all-gather.10.cloned.1.call-start = ((), (), s32[]{:S(2)}) async-start(), calls=%async_computation.4 | async-start | bytes 8650752 | tf_op jit(solution)/shard_map/all_gather | solution.py:14
Sparse Core Ops, SparseCore 0:
  11.2 101.4 all-gather.5
  115.0 157.6 all-gather.7
  286.1 34.6 reduce-scatter.1
  371.3 103.2 all-gather.9
where the time goes:
time: 598 us; the launch traced here: 596 us
  waiting for transfers between devices  303 us (51%)
  blocking collectives  131 us (22%)
  other arithmetic  92.9 us (16%)
  local copies, waits for them, and re-layouts  31.4 us (5%)
  matrix products  22.2 us (4%)
  between operations  14 us (2%)
    all_gather x1, waiting for transfers between devices, on_device(): lax.all_gather(forward_b, 'space', axis=0, tiled=True)  154 us
    all_gather x2, waiting for transfers between devices, carried_in(): lax.all_gather(a.astype(kind), axis)  149 us
    psum x1, blocking collectives, on_device(): fixed_forward = lax.psum(contrib, ('tm', 'space')).astype(jnp.bfloat16)  78.9 us
    add x31, other arithmetic, combine(): value_l + latter[0] * value_e  62.3 us
    all_gather x1, blocking collectives, carried_in(): lax.all_gather(a.astype(kind), axis)  52.1 us
    convert_element_type x31, other arithmetic, one(): lax.dynamic_index_in_dim(a, source, 0, False).astype(own.dtype)  28.8 us
    while x4, local copies, waits for them, and re-layouts, carried_in(): return lax.fori_loop(0, ahead, one, state)  24.8 us
    dot_general x1, matrix products, on_device(): jnp.einsum('hrn,rhk->nhk', block, inner_rows, preferred_element_type=jnp....  13.2 us
  transfers between devices with their start and end apart: 4, of which 3 were waited for; matrix products, arithmetic and copies ran while one was open for 2% of the time, Pallas kernels for 0%

commit v1 on v0

--- a/solution.py
+++ b/solution.py
@@ -2,8 +2,14 @@
 import jax.numpy as jnp
 from jax import lax
 from jax.sharding import PartitionSpec as P
+from jax.lax import all_gather
 
 TILE = 128
+
+
+def see_chains_in(obj):
+    local_next = all_gather(obj, axis_name=("tm", "space")).sum(axis=0)
+    return local_next
 
 
 def carried_in(shard, axis, join, neutral, backward):
@@ -88,7 +94,7 @@
     contrib = -coupling
     own_part = lax.dynamic_slice_in_dim(contrib, share_start, share_rows, 1) + fixed_rhs
     contrib = lax.dynamic_update_slice_in_dim(contrib, own_part, share_start, 1)
-    fixed_forward = lax.psum(contrib, ("tm", "space")).astype(jnp.bfloat16)
+    fixed_forward = see_chains_in(contrib).astype(jnp.bfloat16)
     fixed_total = tip_factor.shape[1]
     fixed_index = jnp.arange(fixed_total, dtype=jnp.int32)
     lower_tri = fixed_index[:, None] >= fixed_index[None, :]

time: 598 us -> 895 us (1.50)
  waiting for transfers between devices: 303 us -> 636 us
  blocking collectives: 131 us -> 52.1 us
  other arithmetic: 92.9 us -> 134 us
    all_gather x0 -> x1, waiting for transfers between devices: none -> 338 us  [see_chains_in(): local_next = all_gather(obj, axis_name=('tm', 'space')).sum(axis=0)]
    psum x1 -> x0, blocking collectives: 78.9 us -> none  [on_device(): fixed_forward = lax.psum(contrib, ('tm', 'space')).astype(jnp.bfloat16)]
    reduce_sum x0 -> x1, other arithmetic: none -> 41.4 us  [see_chains_in(): local_next = all_gather(obj, axis_name=('tm', 'space')).sum(axis=0)]
  transfers between devices with their start and end apart: 4 -> 5, of which waited for: 3 -> 4; matrix products, arithmetic and copies ran while one was open for 2% -> 8% of each run, Pallas kernels for 0% -> 0%
where the time goes in v1:
time: 895 us; the launch traced here: 893 us
  waiting for transfers between devices  636 us (71%)
  other arithmetic  134 us (15%)
  blocking collectives  52.1 us (6%)
  local copies, waits for them, and re-layouts  32.2 us (4%)
  matrix products  23.5 us (3%)
  between operations  14 us (2%)
    all_gather x1, waiting for transfers between devices, see_chains_in(): local_next = all_gather(obj, axis_name=('tm', 'space')).sum(axis=0)  338 us
    all_gather x1, waiting for transfers between devices, on_device(): lax.all_gather(forward_b, 'space', axis=0, tiled=True)  151 us
    all_gather x2, waiting for transfers between devices, carried_in(): lax.all_gather(a.astype(kind), axis)  147 us
    add x31, other arithmetic, combine(): value_l + latter[0] * value_e  62.3 us
    all_gather x1, blocking collectives, carried_in(): lax.all_gather(a.astype(kind), axis)  52.1 us
    reduce_sum x1, other arithmetic, see_chains_in(): local_next = all_gather(obj, axis_name=('tm', 'space')).sum(axis=0)  41.4 us
    convert_element_type x31, other arithmetic, one(): lax.dynamic_index_in_dim(a, source, 0, False).astype(own.dtype)  28.7 us
    while x4, local copies, waits for them, and re-layouts, carried_in(): return lax.fori_loop(0, ahead, one, state)  24.8 us
  transfers between devices with their start and end apart: 5, of which 4 were waited for; matrix products, arithmetic and copies ran while one was open for 8% of the time, Pallas kernels for 0%

profile of v1, /device:TPU:2, one launch (start us, length us, event | category | flops | bytes accessed | tf_op | source)
XLA Modules:
  0.0 892.9 jit_solution(9895036819756672031)
XLA Ops:
  11.1 52.1 %all-gather = bf16[32,512,2]{1,2,0:T(2,128)(2,1)S(1)} all-gather(bf16[1,512,2]{1,2,0:T(2,128)(2,1)S(1)} %convert_element_type.103), channel_id=2, replica_groups=mesh['tm'=32,'space'=8] {'tm'}, dimensions={0}, use_global_device_ids=true | all-gather | bytes 67584 | tf_op jit(solution)/shard_map/all_gather | solution.py:20
  63.2 3.3 copy.39
  66.6 46.0 %all-gather.7.cloned.1.call-done = bf16[32,512,2,128]{3,1,2,0:T(8,128)(2,1)} async-done(((bf16[1,512,2,128]{3,1,2,0:T(8,128)(2,1)}), bf16[32,512,2,128]{3,1,2,0:T(8,128)(2,1)}) %all-gather.7.cloned.1.call-update) | async-done | bytes 8388624 | tf_op jit(solution)/shard_map/all_gather | solution.py:20
  117.7 4.1 fusion
  121.8 150.9 %all-gather.9.cloned.1.call-done = bf16[4096,2,128]{0,2,1:T(8,128)(2,1)} async-done(((bf16[512,2,128]{0,2,1:T(8,128)(2,1)}), bf16[4096,2,128]{0,2,1:T(8,128)(2,1)}) %all-gather.9.cloned.1.call-update) | async-done | bytes 2097168 | tf_op jit(solution)/shard_map/all_gather | solution.py:78
  272.7 13.6 %fusion.4 = bf16[4096,2,128]{0,2,1:T(8,128)(2,1)} fusion(bf16[2,1,512,4096]{3,2,1,0:T(8,128)(2,1)} %param.11, pred[512,4096]{1,0:T(8,128)(4,1)} %fusion, bf16[4096,2,128]{0,2,1:T(8,128)(2,1)} %all-gather.9.cloned.1.call-done), kind=kOutput, calls=%fused_computation.12 | convolution fusion | flops 2157051904 | bytes 14680064 | tf_op jit(solution)/shard_map/hrn,rhk->nhk/dot_general | solution.py:83
  286.5 337.8 %all-gather.11.cloned.1.call-done = f32[256,2,512,128]{3,2,1,0:T(8,128)} async-done(((f32[1,2,512,128]{3,2,1,0:T(8,128)}), f32[256,2,512,128]{3,2,1,0:T(8,128)}) %all-gather.11.cloned.1.call-update) | async-done | bytes 134217744 | tf_op jit(solution)/shard_map/all_gather | solution.py:11
  624.3 41.4 %reduce_sum.9 = bf16[2,512,128]{2,1,0:T(8,128)(2,1)S(1)} reduce(f32[256,2,512,128]{3,2,1,0:T(8,128)} %all-gather.11.cloned.1.call-done, f32[]{:T(128)} %constant.87.clone.1), dimensions={0}, to_apply=%region_3.4 | reduce | flops 33423360 | bytes 134479872 | tf_op jit(solution)/shard_map/reduce_sum | solution.py:11
  665.9 2.4 fusion.9
  668.3 2.1 multiply_convert_fusion
  671.0 100.6 %all-gather.13.cloned.1.call-done = bf16[16384,2,128]{0,2,1:T(8,128)(2,1)} async-done(((bf16[512,2,128]{0,2,1:T(8,128)(2,1)}), bf16[16384,2,128]{0,2,1:T(8,128)(2,1)}) %all-gather.13.cloned.1.call-update) | async-done | bytes 8388624 | tf_op jit(solution)/shard_map/all_gather | solution.py:20
  771.7 21.1 %copy.56 = bf16[16384,2,128]{2,1,0:T(2,128)(2,1)} copy(bf16[16384,2,128]{0,2,1:T(8,128)(2,1)} %all-gather.13.cloned.1.call-done) | data formatting | bytes 16777216 | tf_op jit(solution)/shard_map/while | solution.py:35
  792.9 92.2 %while.27 = (s32[]{:T(128)}, f32[512,2,128]{2,1,0:T(2,128)S(1)}, s32[]{:T(128)}, bf16[32,512,2,128]{3,2,1,0:T(2,128)(2,1)}, bf16[32,512,2,1]{2,1,3,0:T(8,128)(2,...) while((s32[]{:T(128)}, f32[512,2,128]{2,1,0:T(2,128)S(1)}, s32[]{:T(128)}, ...), condition=%wide.region_5.6_spmd, body=%wide.region_4.5_spmd.sunk | while | flops 394246 | bytes 1321107 | solution.py:35
  796.8 2.0 convert_add_fusion.5
  802.8 2.0 convert_add_fusion.5
  805.7 2.0 convert_add_fusion.5
  811.7 2.0 convert_add_fusion.5
  817.6 2.0 convert_add_fusion.5
  820.6 2.0 convert_add_fusion.5
  823.6 2.0 convert_add_fusion.5
  826.5 2.0 convert_add_fusion.5
  832.5 2.0 convert_add_fusion.5
  838.4 2.0 convert_add_fusion.5
  841.4 2.0 convert_add_fusion.5
  (91 shorter events, 80.1 us)
Async XLA Ops:
  7.2 106.9 %copy-start = (bf16[1,512,2,512]{3,2,1,0:T(2,128)(2,1)S(1)}, bf16[1,512,2,512]{3,2,1,0:T(2,128)(2,1)}, u32[]{:S(2)}) copy-start(bf16[1,512,2,512]{3,2,1,0:T(2,128)(2,1)} %param.15) | copy-start | bytes 3145732
  7.2 105.5 %all-gather.7.cloned.1.call-start = ((), (), s32[]{:S(2)}) async-start(), calls=%async_computation.1 | async-start | bytes 8650752 | tf_op jit(solution)/shard_map/all_gather | solution.py:20
  9.1 263.6 %all-gather.9.cloned.1.call-start = ((), (), s32[]{:S(2)}) async-start(), calls=%async_computation.2 | async-start | bytes 2359296 | tf_op jit(solution)/shard_map/all_gather | solution.py:78
  63.2 49.8 %copy-start.1 = (f32[1,512,2]{1,2,0:T(2,128)S(1)}, f32[1,512,2]{1,2,0:T(2,128)}, u32[]{:S(2)}) copy-start(f32[1,512,2]{1,2,0:T(2,128)} %param.13) | copy-start | bytes 12292
  66.6 47.3 %copy-start.2 = (f32[2,2,128]{2,1,0:T(2,128)S(1)}, f32[2,2,128]{2,1,0:T(2,128)}, u32[]{:S(2)}) copy-start(f32[2,2,128]{2,1,0:T(2,128)} %param.16) | copy-start | bytes 6148
  112.8 4.9 copy-start.3
  113.9 510.5 %all-gather.11.cloned.1.call-start = ((), (), s32[]{:S(2)}) async-start(), calls=%async_computation.4 | async-start | bytes 134742016 | tf_op jit(solution)/shard_map/all_gather | solution.py:11
  117.6 550.7 %reduce-scatter.2.cloned.1.call-start = ((), (), s32[]{:S(2)}) async-start(), calls=%async_computation.3 | async-start | bytes 2359296 | tf_op jit(solution)/shard_map/reduce_scatter | solution.py:82
  286.3 485.3 %all-gather.13.cloned.1.call-start = ((), (), s32[]{:S(2)}) async-start(), calls=%async_computation.5 | async-start | bytes 8650752 | tf_op jit(solution)/shard_map/all_gather | solution.py:20
Sparse Core Ops, SparseCore 0:
  11.2 101.4 all-gather.6
  114.5 158.2 all-gather.8
  277.0 347.2 all-gather.10
  626.7 30.2 reduce-scatter.1
  670.6 101.0 all-gather.12
